TPU v7x, 32 devices: a whole 2x2x4 slice. The times are simulated.
32 devices in a mesh: groups: 2 (over y), blk: 4 (over z), rep: 4 (over x, core).
Axes of the slice: x: 2, y: 2, z: 4, core: 2. Of those that a mesh axis runs over, the one named last changes fastest.
Arguments:
- embeddings: float32 [8192, 128], P(('groups', 'blk')), parts along dimension 0, may hold values from -6 to 6
- degrees: int32 [8192], P(('groups', 'blk')), parts along dimension 0, may hold values from 1 to 12800, as said below
- tile_values: bfloat16 [8, 4, 1, 24, 128, 128], P(('groups', 'blk'), 'rep'), parts along dimension 0
- tile_rows: int32 [8, 4, 1, 24], P(('groups', 'blk'), 'rep'), parts along dimension 0, may hold values from 0 to 7
- tile_columns: int32 [8, 4, 1, 24], P(('groups', 'blk'), 'rep'), parts along dimension 0, may hold values from 0 to 7
- slot_counts: int32 [8, 4, 1], P(('groups', 'blk'), 'rep'), parts along dimension 0, may hold values from 6 to 24, as said below
Outputs:
- combined: float32 [8192, 128], P(('groups', 'blk', 'rep')), parts along dimension 0
There are 2 independent parts, one for each index of `groups`. A program takes and returns all parts, laid end to end along the dimension named above; each array names one. Nothing has to cross between parts.
Inputs may be any that keep to these rules, and one draw needn't show every extreme that they name: `degrees`: each node's degree is at least the number of nonzero entries in its row of A. `slot_counts`: some arc position of some device has all 24 slots live in every draw.
All inputs are finite; a program needn't handle non-finite values.
Results may differ from a plain program's by a relative error of at most 0.0003.
Values sent between devices are 32-bit elements; how exact they have to be, the bound alone decides.
A program may use at most 64 MiB of HBM per device.

v0:
```python
import jax
import jax.numpy as jnp
from jax import lax
from jax.sharding import PartitionSpec as P

LAYERS = 2


def shifted_2(shard, axis, by):
    devices = lax.axis_size(axis)
    return lax.ppermute(shard, axis, [(i, (i + by) % devices) for i in range(devices)])


def slot_term(source_panel, arc_slot, slots):
    tile_values, tile_rows, tile_columns, slot_counts = slots
    slot_total = tile_values.shape[1]
    block_total = source_panel.shape[0]
    columns = lax.dynamic_index_in_dim(tile_columns, arc_slot, 0, keepdims=False)
    values = lax.dynamic_index_in_dim(tile_values, arc_slot, 0, keepdims=False)
    row_blocks = lax.dynamic_index_in_dim(tile_rows, arc_slot, 0, keepdims=False)
    live_count = lax.dynamic_index_in_dim(slot_counts, arc_slot, 0, keepdims=False)
    blocks = jnp.take(source_panel, columns, axis=0)
    products = jnp.einsum(
        "jab,jbw->jaw",
        values,
        blocks,
        precision=lax.Precision.HIGHEST,
        preferred_element_type=jnp.float32,
    )
    live_slots = jnp.arange(slot_total, dtype=jnp.int32) < live_count
    placement = (
        (row_blocks[:, None] == jnp.arange(block_total, dtype=jnp.int32)[None, :])
        & live_slots[:, None]
    ).astype(jnp.float32)
    return jnp.einsum("jc,jaw->caw", placement, products, precision=lax.Precision.HIGHEST)


def arc_product(source_panel, slots, team_index, team_count):
    arc_length = slots[0].shape[0]
    arc_panel = source_panel
    for power_index in range(team_count.bit_length() - 1):
        shifted = shifted_2(arc_panel, "blk", arc_length * (1 << power_index))
        arc_panel = jnp.where(team_index >> power_index & 1 == 1, shifted, arc_panel)
    empty = jnp.zeros(source_panel.shape, jnp.float32)

    def walk(arc_slot, loop_state):
        partial_value, panel_now = loop_state
        partial_value = partial_value + slot_term(panel_now, arc_slot, slots)
        panel_now = shifted_2(panel_now, "blk", 1)
        return (partial_value, panel_now)

    partial_value, panel_now = lax.fori_loop(0, arc_length - 1, walk, (empty, arc_panel))
    return partial_value + slot_term(panel_now, arc_length - 1, slots)


def per_device(embeddings, degrees, tile_values, tile_rows, tile_columns, slot_counts):
    tile_size = tile_values.shape[-1]
    width_count = embeddings.shape[1]
    block_count = embeddings.shape[0] // tile_size
    slots = (tile_values[0, 0], tile_rows[0, 0], tile_columns[0, 0], slot_counts[0, 0])
    team_index = lax.axis_index("rep")
    team_count = lax.axis_size("rep")
    share_rows = embeddings.shape[0] // team_count
    norm_scale = lax.rsqrt(degrees.astype(jnp.float32))
    current = embeddings
    combined = lax.dynamic_slice_in_dim(embeddings, team_index * share_rows, share_rows)
    for layer_index in range(LAYERS):
        source_panel = (current * norm_scale[:, None]).reshape(block_count, tile_size, width_count)
        partial_value = arc_product(source_panel, slots, team_index, team_count)
        partial_value = partial_value.reshape(block_count * tile_size, width_count)
        current = lax.psum(partial_value, "rep") * norm_scale[:, None]
        combined = combined + lax.dynamic_slice_in_dim(current, team_index * share_rows, share_rows)
    return combined / (LAYERS + 1.0)


def solution(mesh):
    in_specs = (
        P(("groups", "blk"), None),
        P(("groups", "blk")),
        P(("groups", "blk"), "rep", None, None, None, None),
        P(("groups", "blk"), "rep", None, None),
        P(("groups", "blk"), "rep", None, None),
        P(("groups", "blk"), "rep", None),
    )
    out_specs = P(("groups", "blk", "rep"), None)
    return jax.shard_map(
        per_device, mesh=mesh, in_specs=in_specs, out_specs=out_specs, check_vma=False
    )
```

profile of v0, /device:TPU:0, one launch (start us, length us, event | category | flops | bytes accessed | tf_op | source)
XLA Modules:
  0.0 182.0 jit_solution(11972040666576285834)
XLA Ops:
  6.5 0.0 copy-start
  6.5 0.0 copy-start.2
  6.5 0.0 all-reduce.3.cloned.1.call-start
  6.5 0.8 convert_rsqrt_fusion
  7.3 1.2 broadcast_multiply_fusion.2
  8.6 3.1 %collective-permute-start = (f32[8,128,128]{2,1,0:T(8,128)S(1)}, f32[8,128,128]{2,1,0:T(8,128)S(1)}, u32[]{:S(2)}, u32[]{:S(2)}) collective-permute-start(f32[8,128,128]{2,1,0:T(8,128)S(1)} %bitcast.28), channel_id=1, source_target_pairs={{0,4},{4,8},{8,12},{12,0},{1,5},{5,9},{9,13},{13,1},{2,6},{6,10},{... | collective-permute-start | bytes 1572872 | tf_op jit(solution)/shard_map/ppermute | solution.py:11
  12.3 13.3 %collective-permute-done = f32[8,128,128]{2,1,0:T(8,128)S(1)} collective-permute-done((f32[8,128,128]{2,1,0:T(8,128)S(1)}, f32[8,128,128]{2,1,0:T(8,128)S(1)}, u32[]{:S(2)}, u32[]{:S(2)}) %collective-permute-start) | collective-permute-done | bytes 524320 | tf_op jit(solution)/shard_map/ppermute | solution.py:11
  25.6 0.1 broadcast_select_fusion.1
  25.6 0.8 collective-permute-start.1
  26.4 0.0 copy-done.2
  26.5 23.3 %collective-permute-done.1 = f32[8,128,128]{2,1,0:T(8,128)S(1)} collective-permute-done((f32[8,128,128]{2,1,0:T(8,128)S(1)}, f32[8,128,128]{2,1,0:T(8,128)S(1)}, u32[]{:S(2)}, u32[]{:S(2)}) %collective-permute-start.1) | collective-permute-done | bytes 524320 | tf_op jit(solution)/shard_map/ppermute | solution.py:11
  49.8 0.1 broadcast_select_fusion.3
  49.9 1.8 gather_fusion
  51.6 0.0 copy-done
  51.7 2.9 %fusion.6 = f32[24,128,128]{2,1,0:T(8,128)S(1)} fusion(f32[24,128,128]{2,1,0:T(8,128)} %gather_fusion, bf16[1,1,1,24,128,128]{5,4,3,2,1,0:T(8,128)(2,1)S(1)} %copy-done, pred[24]{0:T(512)(128)(4,1)S(1)} %compare_and_fusion), kind=kOutput, calls=%fused_computation.8 | convolution fusion | flops 604372992 | bytes 3932184 | tf_op jit(solution)/shard_map/jab,jbw->jaw/dot_general | solution.py:23
  54.5 0.0 copy-start.1
  54.6 1.6 copy.9
  56.2 0.0 copy-done.1
  56.2 2.0 %fusion.2 = f32[8,128,128]{2,0,1:T(8,128)S(1)} fusion(f32[24,128,128]{1,0,2:T(8,128)} %copy.9, s32[24]{0:T(128)S(1)} %bitcast.32, pred[24]{0:T(512)(128)(4,1)S(1)} %iota_compare_fusion.1), kind=kOutput, calls=%fused_computation.4 | convolution fusion | flops 37749120 | bytes 2097272 | tf_op jit(solution)/shard_map/jc,jaw->caw/dot_general | solution.py:35
  58.2 0.9 copy.7
  59.1 0.0 all-reduce.3.cloned.1.call-update
  59.1 0.0 all-reduce.5.cloned.1.call-start
  59.2 33.4 %all-reduce.3.cloned.1.call-done = f32[1024,128]{1,0:T(8,128)} async-done(((f32[1024,128]{1,0:T(8,128)}), f32[1024,128]{1,0:T(8,128)}) %all-reduce.3.cloned.1.call-update) | async-done | bytes 524304 | tf_op jit(solution)/shard_map/psum | solution.py:71
  92.6 1.2 broadcast_multiply_fusion.1
  93.8 1.5 collective-permute-start.2
  95.4 12.8 %collective-permute-done.2 = f32[8,128,128]{2,1,0:T(8,128)S(1)} collective-permute-done((f32[8,128,128]{2,1,0:T(8,128)S(1)}, f32[8,128,128]{2,1,0:T(8,128)S(1)}, u32[]{:S(2)}, u32[]{:S(2)}) %collective-permute-start.2) | collective-permute-done | bytes 524320 | tf_op jit(solution)/shard_map/ppermute | solution.py:11
  108.2 0.1 broadcast_select_fusion
  108.3 0.9 collective-permute-start.3
  109.2 22.5 %collective-permute-done.3 = f32[8,128,128]{2,1,0:T(8,128)S(1)} collective-permute-done((f32[8,128,128]{2,1,0:T(8,128)S(1)}, f32[8,128,128]{2,1,0:T(8,128)S(1)}, u32[]{:S(2)}, u32[]{:S(2)}) %collective-permute-start.3) | collective-permute-done | bytes 524320 | tf_op jit(solution)/shard_map/ppermute | solution.py:11
  131.6 0.1 broadcast_select_fusion.2
  131.7 1.8 gather_fusion.1
  133.5 2.9 %fusion.4 = f32[24,128,128]{2,1,0:T(8,128)S(1)} fusion(f32[24,128,128]{2,1,0:T(8,128)} %gather_fusion.1, bf16[1,1,1,24,128,128]{5,4,3,2,1,0:T(8,128)(2,1)S(1)} %copy-done, pred[24]{0:T(512)(128)(4,1)S(1)} %compare_and_fusion), kind=kOutput, calls=%fused_computation.6 | convolution fusion | flops 604372992 | bytes 3932184 | tf_op jit(solution)/shard_map/jab,jbw->jaw/dot_general | solution.py:23
  136.4 1.6 copy.10
  138.0 2.0 %fusion = f32[8,128,128]{2,0,1:T(8,128)S(1)} fusion(f32[24,128,128]{1,0,2:T(8,128)} %copy.10, s32[24]{0:T(128)S(1)} %bitcast.33, pred[24]{0:T(512)(128)(4,1)S(1)} %iota_compare_fusion.1), kind=kOutput, calls=%fused_computation.2 | convolution fusion | flops 37749120 | bytes 2097272 | tf_op jit(solution)/shard_map/jc,jaw->caw/dot_general | solution.py:35
  140.1 0.9 copy.8
  141.0 0.0 all-reduce.5.cloned.1.call-update
  141.0 0.1 dynamic-slice
  141.1 32.4 %all-reduce.5.cloned.1.call-done = f32[1024,128]{1,0:T(8,128)} async-done(((f32[1024,128]{1,0:T(8,128)}), f32[1024,128]{1,0:T(8,128)}) %all-reduce.5.cloned.1.call-update) | async-done | bytes 524304 | tf_op jit(solution)/shard_map/psum | solution.py:71
  173.5 1.7 fusion.15
  (4 shorter events, 0.0 us)
Async XLA Ops:
  6.5 45.1 %copy-start = (bf16[1,1,1,24,128,128]{5,4,3,2,1,0:T(8,128)(2,1)S(1)}, bf16[1,1,1,24,128,128]{5,4,3,2,1,0:T(8,128)(2,1)}, u32[]{:S(2)}) copy-start(bf16[1,1,1,24,128,128]{5,4,3,2,1,0:T(8,128)(2,1)} %param.10) | copy-start | bytes 2359300
  6.5 19.9 %copy-start.2 = (s32[1,1,1,24]{3,2,1,0:T(1,128)S(1)}, s32[1,1,1,24]{3,2,1,0:T(1,128)}, u32[]{:S(2)}) copy-start(s32[1,1,1,24]{3,2,1,0:T(1,128)} %param.12) | copy-start | bytes 292
  6.5 86.1 %all-reduce.3.cloned.1.call-start = ((), (), s32[]{:S(2)}) async-start(), calls=%async_computation | async-start | bytes 1048576 | tf_op jit(solution)/shard_map/psum | solution.py:71
  8.6 17.0 %collective-permute-start = (f32[8,128,128]{2,1,0:T(8,128)S(1)}, f32[8,128,128]{2,1,0:T(8,128)S(1)}, u32[]{:S(2)}, u32[]{:S(2)}) collective-permute-start(f32[8,128,128]{2,1,0:T(8,128)S(1)} %bitcast.28), channel_id=1, source_target_pairs={{0,4},{4,8},{8,12},{12,0},{1,5},{5,9},{9,13},{13,1},{2,6},{6,10},{... | collective-permute-start | bytes 1572872 | tf_op jit(solution)/shard_map/ppermute | solution.py:11
  25.6 24.1 %collective-permute-start.1 = (f32[8,128,128]{2,1,0:T(8,128)S(1)}, f32[8,128,128]{2,1,0:T(8,128)S(1)}, u32[]{:S(2)}, u32[]{:S(2)}) collective-permute-start(f32[8,128,128]{2,1,0:T(8,128)S(1)} %broadcast_select_fusion.1), channel_id=1, source_target_pairs={{0,8},{4,12},{8,0},{12,4},{1,9},{5,13},{9,1},{13,5},{2,10},{6,14},... | collective-permute-start | bytes 1572872 | tf_op jit(solution)/shard_map/ppermute | solution.py:11
  54.5 1.6 copy-start.1
  59.1 114.3 %all-reduce.5.cloned.1.call-start = ((), (), s32[]{:S(2)}) async-start(), calls=%async_computation.1 | async-start | bytes 1048576 | tf_op jit(solution)/shard_map/psum | solution.py:71
  93.8 14.4 %collective-permute-start.2 = (f32[8,128,128]{2,1,0:T(8,128)S(1)}, f32[8,128,128]{2,1,0:T(8,128)S(1)}, u32[]{:S(2)}, u32[]{:S(2)}) collective-permute-start(f32[8,128,128]{2,1,0:T(8,128)S(1)} %bitcast.26), channel_id=1, source_target_pairs={{0,4},{4,8},{8,12},{12,0},{1,5},{5,9},{9,13},{13,1},{2,6},{6,10},{... | collective-permute-start | bytes 1572872 | tf_op jit(solution)/shard_map/ppermute | solution.py:11
  108.3 23.3 %collective-permute-start.3 = (f32[8,128,128]{2,1,0:T(8,128)S(1)}, f32[8,128,128]{2,1,0:T(8,128)S(1)}, u32[]{:S(2)}, u32[]{:S(2)}) collective-permute-start(f32[8,128,128]{2,1,0:T(8,128)S(1)} %broadcast_select_fusion), channel_id=1, source_target_pairs={{0,8},{4,12},{8,0},{12,4},{1,9},{5,13},{9,1},{13,5},{2,10},{6,14},... | collective-permute-start | bytes 1572872 | tf_op jit(solution)/shard_map/ppermute | solution.py:11
Sparse Core Ops, SparseCore 0:
  59.3 33.2 all-reduce.2
  141.1 32.3 all-reduce.4
where the time goes:
time: 182 us
  waiting for transfers between devices  138 us (76%)
  between operations  14.1 us (8%)
  matrix products  9.86 us (5%)
  local copies, waits for them, and re-layouts  8.72 us (5%)
  starting transfers between devices  6.33 us (3%)
  other arithmetic  5.26 us (3%)
    ppermute x4, waiting for transfers between devices, shifted_2(): lax.ppermute(shard, axis, [(i, (i + by) % devices) for i in range(devices)])  71.9 us
    psum x2, waiting for transfers between devices, per_device(): current = lax.psum(partial_value, 'rep') * norm_scale[:, None]  65.8 us
    ppermute x4, starting transfers between devices, shifted_2(): lax.ppermute(shard, axis, [(i, (i + by) % devices) for i in range(devices)])  6.29 us
    dot_general x2, matrix products, slot_term(): jnp.einsum('jab,jbw->jaw', values, blocks, precision=lax.Precision.HIGHES...  5.78 us
    dot_general x2, matrix products, slot_term(): jnp.einsum('jc,jaw->caw', placement, products, precision=lax.Precision.HI...  4.08 us
  transfers between devices with their start and end apart: 6, of which 6 were waited for; matrix products, arithmetic and copies ran while one was open for 0% of the time, Pallas kernels for 0%

commit v1 on v0

--- a/solution.py
+++ b/solution.py
@@ -68,7 +68,7 @@
         source_panel = (current * norm_scale[:, None]).reshape(block_count, tile_size, width_count)
         partial_value = arc_product(source_panel, slots, team_index, team_count)
         partial_value = partial_value.reshape(block_count * tile_size, width_count)
-        current = lax.psum(partial_value, "rep") * norm_scale[:, None]
+        current = jnp.sum(lax.all_gather(partial_value, "rep"), axis=0) * norm_scale[:, None]
         combined = combined + lax.dynamic_slice_in_dim(current, team_index * share_rows, share_rows)
     return combined / (LAYERS + 1.0)
 

time: 182 us -> 166 us (0.912)
  waiting for transfers between devices: 138 us -> 119 us
  other arithmetic: 5.26 us -> 7.79 us
    psum x2 -> x0, waiting for transfers between devices: 65.8 us -> none  [per_device(): current = lax.psum(partial_value, 'rep') * norm_scale[:, None]]
    all_gather x0 -> x2, waiting for transfers between devices: none -> 44.5 us  [per_device(): lax.all_gather(partial_value, 'rep')]
    reduce_sum x0 -> x2, other arithmetic: none -> 3.51 us  [per_device(): jnp.sum(lax.all_gather(partial_value, 'rep'), axis=0) * norm_scale[:, None]]
    ppermute x4, waiting for transfers between devices: 71.9 us -> 74.9 us  [shifted_2(): lax.ppermute(shard, axis, [(i, (i + by) % devices) for i in range(devices)])]
where the time goes in v1:
time: 166 us
  waiting for transfers between devices  119 us (72%)
  between operations  14.1 us (8%)
  matrix products  9.86 us (6%)
  local copies, waits for them, and re-layouts  8.75 us (5%)
  other arithmetic  7.79 us (5%)
  starting transfers between devices  6.13 us (4%)
    ppermute x4, waiting for transfers between devices, shifted_2(): lax.ppermute(shard, axis, [(i, (i + by) % devices) for i in range(devices)])  74.9 us
    all_gather x2, waiting for transfers between devices, per_device(): lax.all_gather(partial_value, 'rep')  44.5 us
    ppermute x4, starting transfers between devices, shifted_2(): lax.ppermute(shard, axis, [(i, (i + by) % devices) for i in range(devices)])  6.08 us
    dot_general x2, matrix products, slot_term(): jnp.einsum('jab,jbw->jaw', values, blocks, precision=lax.Precision.HIGHES...  5.78 us
    dot_general x2, matrix products, slot_term(): jnp.einsum('jc,jaw->caw', placement, products, precision=lax.Precision.HI...  4.07 us
    gather x2, local copies, waits for them, and re-layouts, slot_term(): blocks = jnp.take(source_panel, columns, axis=0)  3.6 us
    reduce_sum x2, other arithmetic, per_device(): jnp.sum(lax.all_gather(partial_value, 'rep'), axis=0) * norm_scale[:, None]  3.51 us
  transfers between devices with their start and end apart: 6, of which 6 were waited for; matrix products, arithmetic and copies ran while one was open for 0% of the time, Pallas kernels for 0%

profile of v1, /device:TPU:0, one launch (start us, length us, event | category | flops | bytes accessed | tf_op | source)
XLA Modules:
  0.0 166.1 jit_solution(12125771435981745924)
XLA Ops:
  6.5 0.0 copy-start
  6.5 0.0 copy-start.2
  6.5 0.0 all-gather.3.cloned.1.call-start
  6.5 0.8 fusion.31
  7.3 1.2 broadcast_multiply_fusion
  8.6 3.1 %collective-permute-start = (f32[8,128,128]{2,1,0:T(8,128)S(1)}, f32[8,128,128]{2,1,0:T(8,128)S(1)}, u32[]{:S(2)}, u32[]{:S(2)}) collective-permute-start(f32[8,128,128]{2,1,0:T(8,128)S(1)} %bitcast.30), channel_id=1, source_target_pairs={{0,4},{4,8},{8,12},{12,0},{1,5},{5,9},{9,13},{13,1},{2,6},{6,10},{... | collective-permute-start | bytes 1572872 | tf_op jit(solution)/shard_map/ppermute | solution.py:11
  12.3 13.3 %collective-permute-done = f32[8,128,128]{2,1,0:T(8,128)S(1)} collective-permute-done((f32[8,128,128]{2,1,0:T(8,128)S(1)}, f32[8,128,128]{2,1,0:T(8,128)S(1)}, u32[]{:S(2)}, u32[]{:S(2)}) %collective-permute-start) | collective-permute-done | bytes 524320 | tf_op jit(solution)/shard_map/ppermute | solution.py:11
  25.6 0.1 broadcast_select_fusion.1
  25.6 0.8 collective-permute-start.1
  26.4 0.0 copy-done.2
  26.5 23.3 %collective-permute-done.1 = f32[8,128,128]{2,1,0:T(8,128)S(1)} collective-permute-done((f32[8,128,128]{2,1,0:T(8,128)S(1)}, f32[8,128,128]{2,1,0:T(8,128)S(1)}, u32[]{:S(2)}, u32[]{:S(2)}) %collective-permute-start.1) | collective-permute-done | bytes 524320 | tf_op jit(solution)/shard_map/ppermute | solution.py:11
  49.8 0.1 broadcast_select_fusion.3
  49.9 1.8 %gather_fusion = f32[24,128,128]{2,1,0:T(8,128)} fusion(f32[8,128,128]{2,1,0:T(8,128)S(1)} %broadcast_select_fusion.3, s32[1024]{0:T(1024)S(1)} %pad_clamp_fusion), kind=kCustom, calls=%fused_computation.clone | custom fusion | bytes 3145824 | tf_op jit(solution)/shard_map/jit(_take)/gather | solution.py:22
  51.6 0.0 copy-done
  51.7 2.9 %fusion.4 = f32[24,128,128]{1,2,0:T(8,128)S(1)} fusion(f32[24,128,128]{2,1,0:T(8,128)} %gather_fusion, bf16[1,1,1,24,128,128]{5,4,3,2,1,0:T(8,128)(2,1)S(1)} %copy-done, pred[24]{0:T(512)(128)(4,1)S(1)} %compare_and_fusion), kind=kOutput, calls=%fused_computation.6 | convolution fusion | flops 604372992 | bytes 3932184 | tf_op jit(solution)/shard_map/jab,jbw->jaw/dot_general | solution.py:23
  54.5 0.0 copy-start.1
  54.6 1.6 copy.14
  56.2 0.0 copy-done.1
  56.2 2.0 %fusion.23 = f32[8,128,128]{2,0,1:T(8,128)S(1)} fusion(f32[24,128,128]{2,0,1:T(8,128)} %copy.14, s32[24]{0:T(128)S(1)} %bitcast.34, pred[24]{0:T(512)(128)(4,1)S(1)} %iota_compare_fusion.1), kind=kOutput, calls=%fused_computation.31 | convolution fusion | flops 37749120 | bytes 2097272 | tf_op jit(solution)/shard_map/jc,jaw->caw/dot_general | solution.py:35
  58.2 0.9 copy.15
  59.1 0.0 all-gather.3.cloned.1.call-update
  59.2 0.0 all-gather.5.cloned.1.call-start
  59.2 22.8 %all-gather.3.cloned.1.call-done = f32[4,1024,128]{2,1,0:T(8,128)} async-done(((f32[1,1024,128]{2,1,0:T(8,128)}), f32[4,1024,128]{2,1,0:T(8,128)}) %all-gather.3.cloned.1.call-update) | async-done | bytes 2097168 | tf_op jit(solution)/shard_map/all_gather | solution.py:71
  82.0 1.8 %reduce_sum.20 = f32[1024,128]{1,0:T(8,128)S(1)} reduce(f32[4,1024,128]{2,1,0:T(8,128)} %all-gather.3.cloned.1.call-done, f32[]{:T(128)} %constant.48.clone.1), dimensions={0}, to_apply=%region_0.2 | reduce | flops 393216 | bytes 2621444 | tf_op jit(solution)/shard_map/reduce_sum | solution.py:71
  83.8 0.2 multiply_multiply_fusion
  84.0 1.5 collective-permute-start.2
  85.5 14.4 %collective-permute-done.2 = f32[8,128,128]{2,1,0:T(8,128)S(1)} collective-permute-done((f32[8,128,128]{2,1,0:T(8,128)S(1)}, f32[8,128,128]{2,1,0:T(8,128)S(1)}, u32[]{:S(2)}, u32[]{:S(2)}) %collective-permute-start.2) | collective-permute-done | bytes 524320 | tf_op jit(solution)/shard_map/ppermute | solution.py:11
  99.9 0.2 broadcast_select_fusion
  100.1 0.7 collective-permute-start.3
  100.8 23.9 %collective-permute-done.3 = f32[8,128,128]{2,1,0:T(8,128)S(1)} collective-permute-done((f32[8,128,128]{2,1,0:T(8,128)S(1)}, f32[8,128,128]{2,1,0:T(8,128)S(1)}, u32[]{:S(2)}, u32[]{:S(2)}) %collective-permute-start.3) | collective-permute-done | bytes 524320 | tf_op jit(solution)/shard_map/ppermute | solution.py:11
  124.7 0.1 broadcast_select_fusion.2
  124.7 1.8 %gather_fusion.1 = f32[24,128,128]{2,1,0:T(8,128)} fusion(f32[8,128,128]{2,1,0:T(8,128)S(1)} %broadcast_select_fusion.2, s32[1024]{0:T(1024)S(1)} %pad_clamp_fusion), kind=kCustom, calls=%fused_computation.1.clone | custom fusion | bytes 3145824 | tf_op jit(solution)/shard_map/jit(_take)/gather | solution.py:22
  126.5 2.9 %fusion.7 = f32[24,128,128]{1,2,0:T(8,128)S(1)} fusion(f32[24,128,128]{2,1,0:T(8,128)} %gather_fusion.1, bf16[1,1,1,24,128,128]{5,4,3,2,1,0:T(8,128)(2,1)S(1)} %copy-done, pred[24]{0:T(512)(128)(4,1)S(1)} %compare_and_fusion), kind=kOutput, calls=%fused_computation.7 | convolution fusion | flops 604372992 | bytes 3932184 | tf_op jit(solution)/shard_map/jab,jbw->jaw/dot_general | solution.py:23
  129.4 1.6 copy.17
  131.1 2.0 %fusion.21 = f32[8,128,128]{2,0,1:T(8,128)S(1)} fusion(f32[24,128,128]{2,0,1:T(8,128)} %copy.17, s32[24]{0:T(128)S(1)} %bitcast.35, pred[24]{0:T(512)(128)(4,1)S(1)} %iota_compare_fusion.1), kind=kOutput, calls=%fused_computation.30 | convolution fusion | flops 37749120 | bytes 2097272 | tf_op jit(solution)/shard_map/jc,jaw->caw/dot_general | solution.py:35
  133.1 0.9 copy.18
  134.0 0.0 all-gather.5.cloned.1.call-update
  134.0 0.1 dynamic-slice
  134.1 21.7 %all-gather.5.cloned.1.call-done = f32[4,1024,128]{2,1,0:T(8,128)} async-done(((f32[1,1024,128]{2,1,0:T(8,128)}), f32[4,1024,128]{2,1,0:T(8,128)}) %all-gather.5.cloned.1.call-update) | async-done | bytes 2097168 | tf_op jit(solution)/shard_map/all_gather | solution.py:71
  155.8 1.8 %reduce_sum.22 = f32[1024,128]{1,0:T(8,128)S(1)} reduce(f32[4,1024,128]{2,1,0:T(8,128)} %all-gather.5.cloned.1.call-done, f32[]{:T(128)} %constant.48.clone.1), dimensions={0}, to_apply=%region_1.3 | reduce | flops 393216 | bytes 2621444 | tf_op jit(solution)/shard_map/reduce_sum | solution.py:71
  157.6 1.7 %fusion.17 = f32[256,128]{1,0:T(8,128)} fusion(f32[1024,128]{1,0:T(8,128)S(1)} %reduce_sum.22, s32[]{:T(128)S(6)} %select_n.45, f32[1024,128]{1,0:T(8,128)S(1)} %reduce_sum.20, f32[1024,128]{1,0:T(8,128)} %param.8, f32[256]{0:T(256)S(1)} %dynamic-slice), kind=kLoop, calls=%fused_computation.22 | loop fusion | flops 163840 | bytes 525316 | tf_op jit(solution)/shard_map/div | solution.py:73
  (4 shorter events, 0.0 us)
Async XLA Ops:
  6.5 45.1 %copy-start = (bf16[1,1,1,24,128,128]{5,4,3,2,1,0:T(8,128)(2,1)S(1)}, bf16[1,1,1,24,128,128]{5,4,3,2,1,0:T(8,128)(2,1)}, u32[]{:S(2)}) copy-start(bf16[1,1,1,24,128,128]{5,4,3,2,1,0:T(8,128)(2,1)} %param.10) | copy-start | bytes 2359300
  6.5 19.9 %copy-start.2 = (s32[1,1,1,24]{3,2,1,0:T(1,128)S(1)}, s32[1,1,1,24]{3,2,1,0:T(1,128)}, u32[]{:S(2)}) copy-start(s32[1,1,1,24]{3,2,1,0:T(1,128)} %param.12) | copy-start | bytes 292
  6.5 75.5 %all-gather.3.cloned.1.call-start = ((), (), s32[]{:S(2)}) async-start(), calls=%async_computation | async-start | bytes 2621440 | tf_op jit(solution)/shard_map/all_gather | solution.py:71
  8.6 17.0 %collective-permute-start = (f32[8,128,128]{2,1,0:T(8,128)S(1)}, f32[8,128,128]{2,1,0:T(8,128)S(1)}, u32[]{:S(2)}, u32[]{:S(2)}) collective-permute-start(f32[8,128,128]{2,1,0:T(8,128)S(1)} %bitcast.30), channel_id=1, source_target_pairs={{0,4},{4,8},{8,12},{12,0},{1,5},{5,9},{9,13},{13,1},{2,6},{6,10},{... | collective-permute-start | bytes 1572872 | tf_op jit(solution)/shard_map/ppermute | solution.py:11
  25.6 24.1 %collective-permute-start.1 = (f32[8,128,128]{2,1,0:T(8,128)S(1)}, f32[8,128,128]{2,1,0:T(8,128)S(1)}, u32[]{:S(2)}, u32[]{:S(2)}) collective-permute-start(f32[8,128,128]{2,1,0:T(8,128)S(1)} %broadcast_select_fusion.1), channel_id=1, source_target_pairs={{0,8},{4,12},{8,0},{12,4},{1,9},{5,13},{9,1},{13,5},{2,10},{6,14},... | collective-permute-start | bytes 1572872 | tf_op jit(solution)/shard_map/ppermute | solution.py:11
  54.5 1.6 copy-start.1
  59.2 96.7 %all-gather.5.cloned.1.call-start = ((), (), s32[]{:S(2)}) async-start(), calls=%async_computation.1 | async-start | bytes 2621440 | tf_op jit(solution)/shard_map/all_gather | solution.py:71
  84.0 15.9 %collective-permute-start.2 = (f32[8,128,128]{2,1,0:T(8,128)S(1)}, f32[8,128,128]{2,1,0:T(8,128)S(1)}, u32[]{:S(2)}, u32[]{:S(2)}) collective-permute-start(f32[8,128,128]{2,1,0:T(8,128)S(1)} %multiply_multiply_fusion), channel_id=1, source_target_pairs={{0,4},{4,8},{8,12},{12,0},{1,5},{5,9},{9,13},{13,1},{2,6},{6,10},{... | collective-permute-start | bytes 1572872 | tf_op jit(solution)/shard_map/ppermute | solution.py:11
  100.1 24.6 %collective-permute-start.3 = (f32[8,128,128]{2,1,0:T(8,128)S(1)}, f32[8,128,128]{2,1,0:T(8,128)S(1)}, u32[]{:S(2)}, u32[]{:S(2)}) collective-permute-start(f32[8,128,128]{2,1,0:T(8,128)S(1)} %broadcast_select_fusion), channel_id=1, source_target_pairs={{0,8},{4,12},{8,0},{12,4},{1,9},{5,13},{9,1},{13,5},{2,10},{6,14},... | collective-permute-start | bytes 1572872 | tf_op jit(solution)/shard_map/ppermute | solution.py:11
Sparse Core Ops, SparseCore 0:
  59.3 22.6 all-gather.2
  134.2 21.6 all-gather.4
